TPU v7x, 256 devices: a whole 4x4x8 slice. The times are simulated.
256 devices in a mesh: space: 128 (over y, z, x), mp: 2 (over core).
Axes of the slice: x: 4, y: 4, z: 8, core: 2. Of those that a mesh axis runs over, the one named last changes fastest.
Arguments:
- points: bfloat16 [262144, 512], P('space'), may hold values from -40 to 40
- curve_rank: int32 [262144], P('space'), may hold values from 0 to 262143, as said below
- patch_counts: int32 [128, 4], P('space'), may hold values from 1 to 1024, 2048 in all within a row
- norm_gain_attn: float32 [512], replicated, may hold values from 0.1 to 1.9
- w_qkv: bfloat16 [3, 512, 512], P(None, None, 'mp'), may hold values from -1.5 to 1.5
- w_out: bfloat16 [512, 512], P('mp'), may hold values from -0.75 to 0.75
- norm_gain_mlp: float32 [512], replicated, may hold values from 0.1 to 1.9
- w_fc1: bfloat16 [512, 2048], P(None, 'mp'), may hold values from -0.25 to 0.25
- w_fc2: bfloat16 [2048, 512], P('mp'), may hold values from -0.1875 to 0.1875
Outputs:
- layer_out: bfloat16 [262144, 512], P('space')
Inputs may be any that keep to these rules, and one draw needn't show every extreme that they name: curve_rank is a permutation; the points of shard a take exactly the positions b * 2048 + a * 16 + m for every owner b and every m below 16. `patch_counts`: each row sums to 2048.
All inputs are finite; a program needn't handle non-finite values.
Results may differ from a plain program's by a relative error of at most 0.0075.
Values may be sent and summed in bfloat16 or wider, within the bound.
A program may use at most 128 MiB of HBM per device.

v0:
```python
import math
import jax
import jax.numpy as jnp
from jax import lax
from jax.sharding import PartitionSpec as P

PATCH = 1024
HDIM = 64
epsilon = 1e-06


def layer_norm(inputs, gain_row):
    values = inputs.astype(jnp.float32)
    average = jnp.mean(values, axis=-1, keepdims=True)
    centred = values - average
    second = jnp.mean(centred * centred, axis=-1, keepdims=True)
    return (centred * lax.rsqrt(second + epsilon) * gain_row).astype(jnp.bfloat16)


def tile_layout(counts, tile_width):
    starts = jnp.cumsum(counts) - counts
    offsets = jnp.arange(tile_width, dtype=jnp.int32)
    usable = offsets[None, :] < counts[:, None]
    source = jnp.where(usable, starts[:, None] + offsets[None, :], 0)
    return (starts, source, usable)


def back_index(starts, length, tile_width):
    places = jnp.arange(length, dtype=jnp.int32)
    covered = starts[None, :] <= places[:, None]
    owning = jnp.sum(covered.astype(jnp.int32), axis=1) - 1
    start_of = jnp.max(jnp.where(covered, starts[None, :], 0), axis=1)
    return owning * tile_width + places - start_of


def attend(queries, key_rows, value_rows, counts):
    length, columns = queries.shape
    head_count = columns // HDIM
    score_scale = 1.0 / math.sqrt(HDIM)
    starts, source, usable = tile_layout(counts, PATCH)

    def one_tile(packed):
        picked, allowed = packed
        tile_q = queries[picked].reshape(PATCH, head_count, HDIM)
        tile_k = key_rows[picked].reshape(PATCH, head_count, HDIM)
        tile_v = value_rows[picked].reshape(PATCH, head_count, HDIM)
        scores = (
            jnp.einsum("qhd,khd->hqk", tile_q, tile_k, preferred_element_type=jnp.float32)
            * score_scale
        )
        scores = jnp.where(allowed[None, None, :], scores, -jnp.inf)
        highest = jnp.max(scores, axis=2, keepdims=True)
        raised = jnp.exp(scores - highest)
        weights = (raised / jnp.sum(raised, axis=2, keepdims=True)).astype(jnp.bfloat16)
        context = jnp.einsum("hqk,khd->qhd", weights, tile_v, preferred_element_type=jnp.float32)
        return context.astype(jnp.bfloat16).reshape(PATCH, columns)

    tile_out = lax.map(one_tile, (source, usable))
    places = back_index(starts, length, PATCH)
    return tile_out.reshape(-1, columns)[places]


def project(arrived, w_qkv):
    queries = jnp.dot(arrived, w_qkv[0], preferred_element_type=jnp.float32).astype(jnp.bfloat16)
    key_rows = jnp.dot(arrived, w_qkv[1], preferred_element_type=jnp.float32).astype(jnp.bfloat16)
    value_rows = jnp.dot(arrived, w_qkv[2], preferred_element_type=jnp.float32).astype(jnp.bfloat16)
    return (queries, key_rows, value_rows)


def body(
    points, curve_rank, patch_counts, norm_gain_attn, w_qkv, w_out, norm_gain_mlp, w_fc1, w_fc2
):
    shards = lax.axis_size("space")
    length, features = points.shape
    cell_rows = length // shards
    half_cols = w_qkv.shape[2]
    own_index = lax.axis_index("space")
    owner_id = curve_rank // length
    within = curve_rank % length - own_index * cell_rows
    slot_of = owner_id * cell_rows + within
    senders = jnp.zeros((length,), jnp.int32).at[slot_of].set(jnp.arange(length, dtype=jnp.int32))
    normed = layer_norm(points, norm_gain_attn)
    ordered_send = normed[senders].reshape(shards, cell_rows, features)
    arrived = lax.all_to_all(
        ordered_send, "space", split_axis=0, concat_axis=0, tiled=True
    ).reshape(length, features)
    queries, key_rows, value_rows = project(arrived, w_qkv)
    context = attend(queries, key_rows, value_rows, patch_counts[0])
    chip_size = lax.axis_size("mp")
    half_rows = length // chip_size
    chip_index = lax.axis_index("mp")
    partial_value = jnp.dot(context, w_out, preferred_element_type=jnp.float32)
    summed = lax.psum_scatter(partial_value, "mp", scatter_dimension=1, tiled=True).astype(
        jnp.bfloat16
    )
    returned = lax.all_to_all(
        summed.reshape(shards, cell_rows, half_cols),
        "space",
        split_axis=0,
        concat_axis=0,
        tiled=True,
    )
    returned = returned.reshape(length, half_cols)[slot_of]
    attn_out = lax.all_gather(returned, "mp", axis=1, tiled=True)
    middle = (points.astype(jnp.float32) + attn_out.astype(jnp.float32)).astype(jnp.bfloat16)
    normed_mlp = layer_norm(middle, norm_gain_mlp)
    hidden = jax.nn.gelu(
        jnp.dot(normed_mlp, w_fc1, preferred_element_type=jnp.float32), approximate=True
    ).astype(jnp.bfloat16)
    summed_mlp = lax.psum_scatter(
        jnp.dot(hidden, w_fc2, preferred_element_type=jnp.float32).astype(jnp.bfloat16),
        "mp",
        scatter_dimension=0,
        tiled=True,
    ).astype(jnp.float32)
    middle_rows = lax.dynamic_slice_in_dim(middle, chip_index * half_rows, half_rows, 0)
    finished = (middle_rows.astype(jnp.float32) + summed_mlp).astype(jnp.bfloat16)
    return lax.all_gather(finished, "mp", axis=0, tiled=True)


def solution(mesh):
    placed = (
        P("space", None),
        P("space"),
        P("space", None),
        P(),
        P(None, None, "mp"),
        P("mp", None),
        P(),
        P(None, "mp"),
        P("mp", None),
    )
    return jax.shard_map(
        body, mesh=mesh, in_specs=placed, out_specs=P("space", None), check_vma=False
    )
```

profile of v0, /device:TPU:1, one launch (start us, length us, event | category | flops | bytes accessed | tf_op | source)
XLA Modules:
  0.0 431.5 jit_solution(8900344260000890417)
XLA Ops:
  11.7 8.0 %scatter_custom_fusion = s32[2048]{0:T(1024)S(1)} fusion(s32[2048]{0:T(1024)S(1)} %get-tuple-element.62, s32[2048]{0:T(1024)S(1)} %iota.14, s32[]{:T(128)} %constant.44.clone.1), kind=kCustom, calls=%fused_computation.92 | custom fusion | bytes 8196 | tf_op jit(solution)/shard_map/scatter | solution.py:81
  21.9 9.2 %gather_fusion.3 = bf16[2048,512]{1,0:T(8,128)(2,1)} fusion(bf16[2048,512]{1,0:T(8,128)(2,1)S(1)} %fusion.25, s32[2048]{0:T(1024)S(1)} %fusion.54), kind=kCustom, calls=%fused_computation.3 | custom fusion | bytes 4202496 | tf_op jit(solution)/shard_map/gather | solution.py:83
  31.1 16.5 %all-to-all-start = ((bf16[128,16,512]{2,1,0:T(8,128)(2,1)}), bf16[128,16,512]{2,1,0:T(8,128)(2,1)S(1)}, u32[]{:S(2)}, u32[]{:S(2)}) async-start(bf16[128,16,512]{2,1,0:T(8,128)(2,1)} %bitcast.73), calls=%async_computation | async-start | bytes 4194304 | tf_op jit(solution)/shard_map/all_to_all | solution.py:84
  48.9 48.0 %all-to-all-done = bf16[128,16,512]{2,1,0:T(8,128)(2,1)S(1)} async-done(((bf16[128,16,512]{2,1,0:T(8,128)(2,1)}), bf16[128,16,512]{2,1,0:T(8,128)(2,1)S(1)}, u32[]{:S(2)}, u32[]{:S(2)}) %all-to-all-start) | async-done | bytes 2097184 | tf_op jit(solution)/shard_map/all_to_all | solution.py:84
  103.2 178.8 %while.10 = (s32[]{:T(128)}, bf16[4,1024,256]{2,1,0:T(8,128)(2,1)}, s32[4,1024]{1,0:T(4,128)S(1)}, bf16[2048,256]{1,0:T(8,128)(2,1)}, pred[4,1024]{1,0:T(4,128)(...) while((s32[]{:T(128)}, bf16[4,1024,256]{2,1,0:T(8,128)(2,1)}, ...), condition=%wide.region_7.8_spmd, body=%wide.region_4.7_spmd.sunk | while | flops 1099174912 | bytes 44105308 | solution.py:58
  103.2 4.9 %gather_fusion.1 = bf16[1024,256]{1,0:T(8,128)(2,1)} fusion(bf16[2048,256]{1,0:T(8,128)(2,1)S(1)} %get-tuple-element.133, s32[1024]{0:T(1024)S(1)} %broadcast_clamp_fusion.4), kind=kCustom, calls=%fused_computation.1.clone.1 | custom fusion | bytes 1052672 | tf_op jit(solution)/shard_map/while/body/eval_jaxpr/gather | solution.py:44
  110.2 4.9 %gather_fusion.2 = bf16[1024,256]{1,0:T(8,128)(2,1)} fusion(bf16[2048,256]{1,0:T(8,128)(2,1)S(1)} %get-tuple-element.134, s32[1024]{0:T(1024)S(1)} %broadcast_clamp_fusion.4), kind=kCustom, calls=%fused_computation.2.clone.1 | custom fusion | bytes 1052672 | tf_op jit(solution)/shard_map/while/body/eval_jaxpr/gather | solution.py:45
  117.3 10.3 %fusion.89 = (f32[4,1024]{1,0:T(4,128)S(1)}, f32[4,1024,1024]{1,2,0:T(8,128)}) fusion(pred[1024]{0:T(1024)(128)(4,1)S(1)} %dynamic-slice_reduce_fusion.2, bf16[1024,4,64]{0,2,1:T(8,128)(2,1)} %bitcast.69, bf16[1024,4,64]{0,2,1:T(8,128)(2,1)} %bitcast.70), kind=kOutput, calls=%fused_computation.103.clone.1 | convolution fusion | flops 553649152 | bytes 17843200 | tf_op jit(solution)/shard_map/while/body/eval_jaxpr/sub | solution.py:53
  127.6 5.9 %gather_fusion = bf16[1024,256]{1,0:T(8,128)(2,1)} fusion(bf16[2048,256]{1,0:T(8,128)(2,1)} %get-tuple-element.131, s32[1024]{0:T(1024)S(1)} %broadcast_clamp_fusion.4), kind=kCustom, calls=%fused_computation.clone.1 | custom fusion | bytes 1052672 | tf_op jit(solution)/shard_map/while/body/eval_jaxpr/gather | solution.py:46
  135.6 8.4 %fusion.90 = bf16[4,64,1024]{2,1,0:T(8,128)(2,1)} fusion(bf16[1024,4,64]{0,2,1:T(8,128)(2,1)} %bitcast.71, f32[4,1024,1024]{1,2,0:T(8,128)} %get-tuple-element.110, f32[4,1024]{1,0:T(4,128)S(1)} %get-tuple-element.111), kind=kOutput, calls=%fused_computation.17.clone.1 | convolution fusion | flops 545521664 | bytes 17842176 | tf_op jit(solution)/shard_map/while/body/eval_jaxpr/hqk,khd->qhd/dot_general | solution.py:55
  147.9 4.9 %gather_fusion.1 = bf16[1024,256]{1,0:T(8,128)(2,1)} fusion(bf16[2048,256]{1,0:T(8,128)(2,1)S(1)} %get-tuple-element.133, s32[1024]{0:T(1024)S(1)} %broadcast_clamp_fusion.4), kind=kCustom, calls=%fused_computation.1.clone.1 | custom fusion | bytes 1052672 | tf_op jit(solution)/shard_map/while/body/eval_jaxpr/gather | solution.py:44
  154.9 4.9 %gather_fusion.2 = bf16[1024,256]{1,0:T(8,128)(2,1)} fusion(bf16[2048,256]{1,0:T(8,128)(2,1)S(1)} %get-tuple-element.134, s32[1024]{0:T(1024)S(1)} %broadcast_clamp_fusion.4), kind=kCustom, calls=%fused_computation.2.clone.1 | custom fusion | bytes 1052672 | tf_op jit(solution)/shard_map/while/body/eval_jaxpr/gather | solution.py:45
  162.0 10.3 %fusion.89 = (f32[4,1024]{1,0:T(4,128)S(1)}, f32[4,1024,1024]{1,2,0:T(8,128)}) fusion(pred[1024]{0:T(1024)(128)(4,1)S(1)} %dynamic-slice_reduce_fusion.2, bf16[1024,4,64]{0,2,1:T(8,128)(2,1)} %bitcast.69, bf16[1024,4,64]{0,2,1:T(8,128)(2,1)} %bitcast.70), kind=kOutput, calls=%fused_computation.103.clone.1 | convolution fusion | flops 553649152 | bytes 17843200 | tf_op jit(solution)/shard_map/while/body/eval_jaxpr/sub | solution.py:53
  172.3 5.9 %gather_fusion = bf16[1024,256]{1,0:T(8,128)(2,1)} fusion(bf16[2048,256]{1,0:T(8,128)(2,1)} %get-tuple-element.131, s32[1024]{0:T(1024)S(1)} %broadcast_clamp_fusion.4), kind=kCustom, calls=%fused_computation.clone.1 | custom fusion | bytes 1052672 | tf_op jit(solution)/shard_map/while/body/eval_jaxpr/gather | solution.py:46
  180.3 8.4 %fusion.90 = bf16[4,64,1024]{2,1,0:T(8,128)(2,1)} fusion(bf16[1024,4,64]{0,2,1:T(8,128)(2,1)} %bitcast.71, f32[4,1024,1024]{1,2,0:T(8,128)} %get-tuple-element.110, f32[4,1024]{1,0:T(4,128)S(1)} %get-tuple-element.111), kind=kOutput, calls=%fused_computation.17.clone.1 | convolution fusion | flops 545521664 | bytes 17842176 | tf_op jit(solution)/shard_map/while/body/eval_jaxpr/hqk,khd->qhd/dot_general | solution.py:55
  192.6 4.9 %gather_fusion.1 = bf16[1024,256]{1,0:T(8,128)(2,1)} fusion(bf16[2048,256]{1,0:T(8,128)(2,1)S(1)} %get-tuple-element.133, s32[1024]{0:T(1024)S(1)} %broadcast_clamp_fusion.4), kind=kCustom, calls=%fused_computation.1.clone.1 | custom fusion | bytes 1052672 | tf_op jit(solution)/shard_map/while/body/eval_jaxpr/gather | solution.py:44
  206.7 10.3 %fusion.89 = (f32[4,1024]{1,0:T(4,128)S(1)}, f32[4,1024,1024]{1,2,0:T(8,128)}) fusion(pred[1024]{0:T(1024)(128)(4,1)S(1)} %dynamic-slice_reduce_fusion.2, bf16[1024,4,64]{0,2,1:T(8,128)(2,1)} %bitcast.69, bf16[1024,4,64]{0,2,1:T(8,128)(2,1)} %bitcast.70), kind=kOutput, calls=%fused_computation.103.clone.1 | convolution fusion | flops 553649152 | bytes 17843200 | tf_op jit(solution)/shard_map/while/body/eval_jaxpr/sub | solution.py:53
  217.0 5.9 %gather_fusion = bf16[1024,256]{1,0:T(8,128)(2,1)} fusion(bf16[2048,256]{1,0:T(8,128)(2,1)} %get-tuple-element.131, s32[1024]{0:T(1024)S(1)} %broadcast_clamp_fusion.4), kind=kCustom, calls=%fused_computation.clone.1 | custom fusion | bytes 1052672 | tf_op jit(solution)/shard_map/while/body/eval_jaxpr/gather | solution.py:46
  225.0 8.4 %fusion.90 = bf16[4,64,1024]{2,1,0:T(8,128)(2,1)} fusion(bf16[1024,4,64]{0,2,1:T(8,128)(2,1)} %bitcast.71, f32[4,1024,1024]{1,2,0:T(8,128)} %get-tuple-element.110, f32[4,1024]{1,0:T(4,128)S(1)} %get-tuple-element.111), kind=kOutput, calls=%fused_computation.17.clone.1 | convolution fusion | flops 545521664 | bytes 17842176 | tf_op jit(solution)/shard_map/while/body/eval_jaxpr/hqk,khd->qhd/dot_general | solution.py:55
  237.3 4.9 %gather_fusion.1 = bf16[1024,256]{1,0:T(8,128)(2,1)} fusion(bf16[2048,256]{1,0:T(8,128)(2,1)S(1)} %get-tuple-element.133, s32[1024]{0:T(1024)S(1)} %broadcast_clamp_fusion.4), kind=kCustom, calls=%fused_computation.1.clone.1 | custom fusion | bytes 1052672 | tf_op jit(solution)/shard_map/while/body/eval_jaxpr/gather | solution.py:44
  244.3 4.9 %gather_fusion.2 = bf16[1024,256]{1,0:T(8,128)(2,1)} fusion(bf16[2048,256]{1,0:T(8,128)(2,1)S(1)} %get-tuple-element.134, s32[1024]{0:T(1024)S(1)} %broadcast_clamp_fusion.4), kind=kCustom, calls=%fused_computation.2.clone.1 | custom fusion | bytes 1052672 | tf_op jit(solution)/shard_map/while/body/eval_jaxpr/gather | solution.py:45
  251.4 10.3 %fusion.89 = (f32[4,1024]{1,0:T(4,128)S(1)}, f32[4,1024,1024]{1,2,0:T(8,128)}) fusion(pred[1024]{0:T(1024)(128)(4,1)S(1)} %dynamic-slice_reduce_fusion.2, bf16[1024,4,64]{0,2,1:T(8,128)(2,1)} %bitcast.69, bf16[1024,4,64]{0,2,1:T(8,128)(2,1)} %bitcast.70), kind=kOutput, calls=%fused_computation.103.clone.1 | convolution fusion | flops 553649152 | bytes 17843200 | tf_op jit(solution)/shard_map/while/body/eval_jaxpr/sub | solution.py:53
  261.7 5.9 %gather_fusion = bf16[1024,256]{1,0:T(8,128)(2,1)} fusion(bf16[2048,256]{1,0:T(8,128)(2,1)} %get-tuple-element.131, s32[1024]{0:T(1024)S(1)} %broadcast_clamp_fusion.4), kind=kCustom, calls=%fused_computation.clone.1 | custom fusion | bytes 1052672 | tf_op jit(solution)/shard_map/while/body/eval_jaxpr/gather | solution.py:46
  269.7 8.4 %fusion.90 = bf16[4,64,1024]{2,1,0:T(8,128)(2,1)} fusion(bf16[1024,4,64]{0,2,1:T(8,128)(2,1)} %bitcast.71, f32[4,1024,1024]{1,2,0:T(8,128)} %get-tuple-element.110, f32[4,1024]{1,0:T(4,128)S(1)} %get-tuple-element.111), kind=kOutput, calls=%fused_computation.17.clone.1 | convolution fusion | flops 545521664 | bytes 17842176 | tf_op jit(solution)/shard_map/while/body/eval_jaxpr/hqk,khd->qhd/dot_general | solution.py:55
  282.0 8.5 %gather_fusion.4 = bf16[2048,256]{1,0:T(8,128)(2,1)S(1)} fusion(bf16[4096,256]{1,0:T(8,128)(2,1)} %bitcast.68, s32[2048]{0:T(1024)S(1)} %copy-done.5), kind=kCustom, calls=%fused_computation.4 | custom fusion | bytes 2105344 | tf_op jit(solution)/shard_map/gather | solution.py:60
  293.3 15.8 %reduce-scatter.3.cloned.1.call-done = f32[2048,256]{1,0:T(8,128)} async-done(((f32[2048,512]{1,0:T(8,128)}), f32[2048,256]{1,0:T(8,128)}) %reduce-scatter.3.cloned.1.call-update) | async-done | bytes 2097168 | tf_op jit(solution)/shard_map/reduce_scatter | solution.py:93
  310.8 40.7 %all_to_all.10 = bf16[128,16,256]{2,1,0:T(8,128)(2,1)S(1)} all-to-all(bf16[128,16,256]{2,1,0:T(8,128)(2,1)S(1)} %bitcast.74), channel_id=1, replica_groups=mesh['space'=128,'mp'=2] {'space'}, dimensions={0} | all-to-all | bytes 2097152 | tf_op jit(solution)/shard_map/all_to_all | solution.py:96
  351.5 9.1 %gather_fusion.5 = bf16[2048,256]{1,0:T(8,128)(2,1)} fusion(bf16[2048,256]{1,0:T(8,128)(2,1)S(1)} %bitcast.67, s32[2048]{0:T(1024)S(1)} %copy-done.4), kind=kCustom, calls=%fused_computation.5 | custom fusion | bytes 2105344 | tf_op jit(solution)/shard_map/gather | solution.py:103
  360.9 13.2 %all-gather.6.cloned.1.call-done = bf16[2048,512]{1,0:T(8,128)(2,1)} async-done(((bf16[2048,256]{1,0:T(8,128)(2,1)}), bf16[2048,512]{1,0:T(8,128)(2,1)}) %all-gather.6.cloned.1.call-update) | async-done | bytes 2097168 | tf_op jit(solution)/shard_map/all_gather | solution.py:104
  378.1 7.3 %fusion.32 = bf16[2048,512]{1,0:T(8,128)(2,1)} fusion(bf16[1024,512]{1,0:T(8,128)(2,1)S(1)} %copy-done, bf16[512,1024]{1,0:T(8,128)(2,1)} %param.18, bf16[2048,512]{1,0:T(8,128)(2,1)S(1)} %get-tuple-element.60, f32[512]{0:T(512)S(1)} %copy-done.10, f32[2048]{0:T(1024)S(1)} %add_rsqrt_fusion, f32[2048]{0:T(1024)S(1)} %broadcast_multiply_fusion), kind=kOutput, calls=%fused_computation.50 | convolution fusion | flops 4320133120 | bytes 6309888 | tf_op jit(solution)/shard_map/dot_general | solution.py:111
  385.5 16.1 %reduce-scatter.5.cloned.1.call-done = bf16[1024,512]{1,0:T(8,128)(2,1)} async-done(((bf16[2048,512]{1,0:T(8,128)(2,1)}), bf16[1024,512]{1,0:T(8,128)(2,1)}) %reduce-scatter.5.cloned.1.call-update) | async-done | bytes 1048592 | tf_op jit(solution)/shard_map/reduce_scatter | solution.py:110
  404.0 17.9 %all-gather.4.cloned.1.call-done = bf16[2048,512]{1,0:T(8,128)(2,1)} async-done(((bf16[1024,512]{1,0:T(8,128)(2,1)}), bf16[2048,512]{1,0:T(8,128)(2,1)}) %all-gather.4.cloned.1.call-update) | async-done | bytes 2097168 | tf_op jit(solution)/shard_map/all_gather | solution.py:118
  (92 shorter events, 74.7 us)
Async XLA Ops:
  6.5 371.6 %copy-start = (bf16[1024,512]{1,0:T(8,128)(2,1)S(1)}, bf16[1024,512]{1,0:T(8,128)(2,1)}, u32[]{:S(2)}) copy-start(bf16[1024,512]{1,0:T(8,128)(2,1)} %param.19) | copy-start | bytes 3145732
  6.5 4.5 %copy-start.6 = (s32[2048]{0:T(1024)S(1)}, s32[2048]{0:T(1024)}, u32[]{:S(2)}) copy-start(s32[2048]{0:T(1024)} %param.12) | copy-start | bytes 24580
  6.5 13.2 %copy-start.7 = (f32[512]{0:T(512)S(1)}, f32[512]{0:T(512)}, u32[]{:S(2)}) copy-start(f32[512]{0:T(512)} %param.14) | copy-start | bytes 6148
  31.1 16.7 %copy-start.8 = (s32[1,4]{1,0:T(1,128)S(1)}, s32[1,4]{1,0:T(1,128)}, u32[]{:S(2)}) copy-start(s32[1,4]{1,0:T(1,128)} %param.13) | copy-start | bytes 52
  31.1 65.8 %all-to-all-start = ((bf16[128,16,512]{2,1,0:T(8,128)(2,1)}), bf16[128,16,512]{2,1,0:T(8,128)(2,1)S(1)}, u32[]{:S(2)}, u32[]{:S(2)}) async-start(bf16[128,16,512]{2,1,0:T(8,128)(2,1)} %bitcast.73), calls=%async_computation | async-start | bytes 4194304 | tf_op jit(solution)/shard_map/all_to_all | solution.py:84
  47.5 261.6 %reduce-scatter.3.cloned.1.call-start = ((), (), s32[]{:S(2)}) async-start(), calls=%async_computation.4 | async-start | bytes 6291456 | tf_op jit(solution)/shard_map/reduce_scatter | solution.py:93
  96.9 1.4 copy-start.1
  98.2 2.5 copy-start.9
  98.2 2.6 copy-start.2
  103.2 178.8 %copy-start.5 = (s32[2048]{0:T(1024)S(1)}, s32[2048]{0:T(1024)}, u32[]{:S(2)}) copy-start(s32[2048]{0:T(1024)} %broadcast_clamp_fusion.1) | copy-start | bytes 24580
  282.0 8.6 %copy-start.3 = (bf16[256,512]{1,0:T(8,128)(2,1)S(1)}, bf16[256,512]{1,0:T(8,128)(2,1)}, u32[]{:S(2)}) copy-start(bf16[256,512]{1,0:T(8,128)(2,1)} %param.16) | copy-start | bytes 786436
  293.2 58.3 %copy-start.4 = (s32[2048]{0:T(1024)S(1)}, s32[2048]{0:T(1024)}, u32[]{:S(2)}) copy-start(s32[2048]{0:T(1024)} %get-tuple-element.61) | copy-start | bytes 24580
  293.2 80.9 %all-gather.6.cloned.1.call-start = ((), (), s32[]{:S(2)}) async-start(), calls=%async_computation.7 | async-start | bytes 3145728 | tf_op jit(solution)/shard_map/all_gather | solution.py:104
  360.6 17.5 %copy-start.10 = (f32[512]{0:T(512)S(1)}, f32[512]{0:T(512)}, u32[]{:S(2)}) copy-start(f32[512]{0:T(512)} %param.17) | copy-start | bytes 6148
  360.6 40.9 %reduce-scatter.5.cloned.1.call-start = ((), (), s32[]{:S(2)}) async-start(), calls=%async_computation.5 | async-start | bytes 3145728 | tf_op jit(solution)/shard_map/reduce_scatter | solution.py:110
  385.4 36.5 %all-gather.4.cloned.1.call-start = ((), (), s32[]{:S(2)}) async-start(), calls=%async_computation.6 | async-start | bytes 3145728 | tf_op jit(solution)/shard_map/all_gather | solution.py:118
Sparse Core Ops, SparseCore 0:
  293.4 15.7 reduce-scatter.2
  360.7 13.3 all-gather.5
  385.5 15.9 reduce-scatter.4
  404.2 17.7 all-gather.3
where the time goes:
time: 433 us; the launch traced here: 432 us
  local copies, waits for them, and re-layouts  143 us (33%)
  waiting for transfers between devices  111 us (26%)
  matrix products  89.6 us (21%)
  blocking collectives  40.7 us (9%)
  starting transfers between devices  17 us (4%)
  other arithmetic  16.5 us (4%)
  between operations  13.3 us (3%)
    all_to_all x1, waiting for transfers between devices, body(): lax.all_to_all(ordered_send, 'space', split_axis=0, concat_axis=0, tiled=...  48 us
    sub x4, matrix products, one_tile(): raised = jnp.exp(scores - highest)  41.4 us
    all_to_all x1, blocking collectives, body(): lax.all_to_all(summed.reshape(shards, cell_rows, half_cols), 'space', spl...  40.7 us
    dot_general x4, matrix products, one_tile(): jnp.einsum('hqk,khd->qhd', weights, tile_v, preferred_element_type=jnp.fl...  33.5 us
    gather x8, local copies, waits for them, and re-layouts, one_tile(): tile_v = value_rows[picked].reshape(PATCH, head_count, HDIM)  32 us
    gather x8, local copies, waits for them, and re-layouts, one_tile(): tile_q = queries[picked].reshape(PATCH, head_count, HDIM)  28.1 us
    gather x8, local copies, waits for them, and re-layouts, one_tile(): tile_k = key_rows[picked].reshape(PATCH, head_count, HDIM)  28 us
    all_gather x1, waiting for transfers between devices, body(): return lax.all_gather(finished, 'mp', axis=0, tiled=True)  17.9 us
  transfers between devices with their start and end apart: 5, of which 5 were waited for; matrix products, arithmetic and copies ran while one was open for 0% of the time, Pallas kernels for 0%

commit v1 on v0

--- a/solution.py
+++ b/solution.py
@@ -101,7 +101,9 @@
         tiled=True,
     )
     returned = returned.reshape(length, half_cols)[slot_of]
-    attn_out = lax.all_gather(returned, "mp", axis=1, tiled=True)
+    attn_out = jnp.concatenate(
+        lax.all_to_all(jnp.stack([returned] * lax.axis_size("mp")), "mp", 0, 0), axis=1
+    )
     middle = (points.astype(jnp.float32) + attn_out.astype(jnp.float32)).astype(jnp.bfloat16)
     normed_mlp = layer_norm(middle, norm_gain_mlp)
     hidden = jax.nn.gelu(

time: 433 us -> 420 us (0.970)
  waiting for transfers between devices: 111 us -> 91.4 us
  blocking collectives: 40.7 us -> 49.2 us
    all_gather x1 -> x0, waiting for transfers between devices: 13.2 us -> none  [body(): attn_out = lax.all_gather(returned, 'mp', axis=1, tiled=True)]
    all_to_all x0 -> x1, blocking collectives: none -> 8.47 us  [body(): lax.all_to_all(jnp.stack([returned] * lax.axis_size('mp')), 'mp', 0, 0)]
    reduce_scatter x1, waiting for transfers between devices: 16.1 us -> 9.61 us  [body(): lax.psum_scatter(jnp.dot(hidden, w_fc2, preferred_element_type=jnp.float3...]
  transfers between devices with their start and end apart: 5 -> 4, of which waited for: 5 -> 4; matrix products, arithmetic and copies ran while one was open for 0% -> 0% of each run, Pallas kernels for 0% -> 0%
where the time goes in v1:
time: 420 us; the launch traced here: 418 us
  local copies, waits for them, and re-layouts  143 us (34%)
  waiting for transfers between devices  91.4 us (22%)
  matrix products  89.6 us (21%)
  blocking collectives  49.2 us (12%)
  starting transfers between devices  16.8 us (4%)
  other arithmetic  14.6 us (3%)
  between operations  13.4 us (3%)
    all_to_all x1, waiting for transfers between devices, body(): lax.all_to_all(ordered_send, 'space', split_axis=0, concat_axis=0, tiled=...  48 us
    sub x4, matrix products, one_tile(): raised = jnp.exp(scores - highest)  41.4 us
    all_to_all x1, blocking collectives, body(): lax.all_to_all(summed.reshape(shards, cell_rows, half_cols), 'space', spl...  40.7 us
    dot_general x4, matrix products, one_tile(): jnp.einsum('hqk,khd->qhd', weights, tile_v, preferred_element_type=jnp.fl...  33.5 us
    gather x8, local copies, waits for them, and re-layouts, one_tile(): tile_v = value_rows[picked].reshape(PATCH, head_count, HDIM)  32 us
    gather x8, local copies, waits for them, and re-layouts, one_tile(): tile_q = queries[picked].reshape(PATCH, head_count, HDIM)  28.1 us
    gather x8, local copies, waits for them, and re-layouts, one_tile(): tile_k = key_rows[picked].reshape(PATCH, head_count, HDIM)  28 us
    all_gather x1, waiting for transfers between devices, body(): return lax.all_gather(finished, 'mp', axis=0, tiled=True)  17.9 us
  transfers between devices with their start and end apart: 4, of which 4 were waited for; matrix products, arithmetic and copies ran while one was open for 0% of the time, Pallas kernels for 0%

profile of v1, /device:TPU:1, one launch (start us, length us, event | category | flops | bytes accessed | tf_op | source)
XLA Modules:
  0.0 418.2 jit_solution(12342200251017675027)
XLA Ops:
  11.7 8.0 %scatter_custom_fusion = s32[2048]{0:T(1024)S(1)} fusion(s32[2048]{0:T(1024)S(1)} %get-tuple-element.62, s32[2048]{0:T(1024)S(1)} %iota.14, s32[]{:T(128)} %constant.44.clone.1), kind=kCustom, calls=%fused_computation.94 | custom fusion | bytes 8196 | tf_op jit(solution)/shard_map/scatter | solution.py:81
  21.9 9.2 %gather_fusion.3 = bf16[2048,512]{1,0:T(8,128)(2,1)} fusion(bf16[2048,512]{1,0:T(8,128)(2,1)S(1)} %fusion.25, s32[2048]{0:T(1024)S(1)} %fusion.54), kind=kCustom, calls=%fused_computation.3 | custom fusion | bytes 4202496 | tf_op jit(solution)/shard_map/gather | solution.py:83
  31.1 16.5 %all-to-all-start = ((bf16[128,16,512]{2,1,0:T(8,128)(2,1)}), bf16[128,16,512]{2,1,0:T(8,128)(2,1)S(1)}, u32[]{:S(2)}, u32[]{:S(2)}) async-start(bf16[128,16,512]{2,1,0:T(8,128)(2,1)} %bitcast.79), calls=%async_computation | async-start | bytes 4194304 | tf_op jit(solution)/shard_map/all_to_all | solution.py:84
  48.9 48.0 %all-to-all-done = bf16[128,16,512]{2,1,0:T(8,128)(2,1)S(1)} async-done(((bf16[128,16,512]{2,1,0:T(8,128)(2,1)}), bf16[128,16,512]{2,1,0:T(8,128)(2,1)S(1)}, u32[]{:S(2)}, u32[]{:S(2)}) %all-to-all-start) | async-done | bytes 2097184 | tf_op jit(solution)/shard_map/all_to_all | solution.py:84
  103.2 178.8 %while.10 = (s32[]{:T(128)}, bf16[4,1024,256]{2,1,0:T(8,128)(2,1)}, s32[4,1024]{1,0:T(4,128)S(1)}, bf16[2048,256]{1,0:T(8,128)(2,1)}, pred[4,1024]{1,0:T(4,128)(...) while((s32[]{:T(128)}, bf16[4,1024,256]{2,1,0:T(8,128)(2,1)}, ...), condition=%wide.region_7.8_spmd, body=%wide.region_4.7_spmd.sunk | while | flops 1099174912 | bytes 44105308 | solution.py:58
  103.2 4.9 %gather_fusion.1 = bf16[1024,256]{1,0:T(8,128)(2,1)} fusion(bf16[2048,256]{1,0:T(8,128)(2,1)S(1)} %get-tuple-element.133, s32[1024]{0:T(1024)S(1)} %broadcast_clamp_fusion.4), kind=kCustom, calls=%fused_computation.1.clone.1 | custom fusion | bytes 1052672 | tf_op jit(solution)/shard_map/while/body/eval_jaxpr/gather | solution.py:44
  110.2 4.9 %gather_fusion.2 = bf16[1024,256]{1,0:T(8,128)(2,1)} fusion(bf16[2048,256]{1,0:T(8,128)(2,1)S(1)} %get-tuple-element.134, s32[1024]{0:T(1024)S(1)} %broadcast_clamp_fusion.4), kind=kCustom, calls=%fused_computation.2.clone.1 | custom fusion | bytes 1052672 | tf_op jit(solution)/shard_map/while/body/eval_jaxpr/gather | solution.py:45
  117.3 10.3 %fusion.89 = (f32[4,1024]{1,0:T(4,128)S(1)}, f32[4,1024,1024]{1,2,0:T(8,128)}) fusion(pred[1024]{0:T(1024)(128)(4,1)S(1)} %dynamic-slice_reduce_fusion.2, bf16[1024,4,64]{0,2,1:T(8,128)(2,1)} %bitcast.75, bf16[1024,4,64]{0,2,1:T(8,128)(2,1)} %bitcast.76), kind=kOutput, calls=%fused_computation.105.clone.1 | convolution fusion | flops 553649152 | bytes 17843200 | tf_op jit(solution)/shard_map/while/body/eval_jaxpr/sub | solution.py:53
  127.6 5.9 %gather_fusion = bf16[1024,256]{1,0:T(8,128)(2,1)} fusion(bf16[2048,256]{1,0:T(8,128)(2,1)} %get-tuple-element.131, s32[1024]{0:T(1024)S(1)} %broadcast_clamp_fusion.4), kind=kCustom, calls=%fused_computation.clone.1 | custom fusion | bytes 1052672 | tf_op jit(solution)/shard_map/while/body/eval_jaxpr/gather | solution.py:46
  135.6 8.4 %fusion.90 = bf16[4,64,1024]{2,1,0:T(8,128)(2,1)} fusion(bf16[1024,4,64]{0,2,1:T(8,128)(2,1)} %bitcast.77, f32[4,1024,1024]{1,2,0:T(8,128)} %get-tuple-element.110, f32[4,1024]{1,0:T(4,128)S(1)} %get-tuple-element.111), kind=kOutput, calls=%fused_computation.17.clone.1 | convolution fusion | flops 545521664 | bytes 17842176 | tf_op jit(solution)/shard_map/while/body/eval_jaxpr/hqk,khd->qhd/dot_general | solution.py:55
  147.9 4.9 %gather_fusion.1 = bf16[1024,256]{1,0:T(8,128)(2,1)} fusion(bf16[2048,256]{1,0:T(8,128)(2,1)S(1)} %get-tuple-element.133, s32[1024]{0:T(1024)S(1)} %broadcast_clamp_fusion.4), kind=kCustom, calls=%fused_computation.1.clone.1 | custom fusion | bytes 1052672 | tf_op jit(solution)/shard_map/while/body/eval_jaxpr/gather | solution.py:44
  154.9 4.9 %gather_fusion.2 = bf16[1024,256]{1,0:T(8,128)(2,1)} fusion(bf16[2048,256]{1,0:T(8,128)(2,1)S(1)} %get-tuple-element.134, s32[1024]{0:T(1024)S(1)} %broadcast_clamp_fusion.4), kind=kCustom, calls=%fused_computation.2.clone.1 | custom fusion | bytes 1052672 | tf_op jit(solution)/shard_map/while/body/eval_jaxpr/gather | solution.py:45
  162.0 10.3 %fusion.89 = (f32[4,1024]{1,0:T(4,128)S(1)}, f32[4,1024,1024]{1,2,0:T(8,128)}) fusion(pred[1024]{0:T(1024)(128)(4,1)S(1)} %dynamic-slice_reduce_fusion.2, bf16[1024,4,64]{0,2,1:T(8,128)(2,1)} %bitcast.75, bf16[1024,4,64]{0,2,1:T(8,128)(2,1)} %bitcast.76), kind=kOutput, calls=%fused_computation.105.clone.1 | convolution fusion | flops 553649152 | bytes 17843200 | tf_op jit(solution)/shard_map/while/body/eval_jaxpr/sub | solution.py:53
  172.3 5.9 %gather_fusion = bf16[1024,256]{1,0:T(8,128)(2,1)} fusion(bf16[2048,256]{1,0:T(8,128)(2,1)} %get-tuple-element.131, s32[1024]{0:T(1024)S(1)} %broadcast_clamp_fusion.4), kind=kCustom, calls=%fused_computation.clone.1 | custom fusion | bytes 1052672 | tf_op jit(solution)/shard_map/while/body/eval_jaxpr/gather | solution.py:46
  180.3 8.4 %fusion.90 = bf16[4,64,1024]{2,1,0:T(8,128)(2,1)} fusion(bf16[1024,4,64]{0,2,1:T(8,128)(2,1)} %bitcast.77, f32[4,1024,1024]{1,2,0:T(8,128)} %get-tuple-element.110, f32[4,1024]{1,0:T(4,128)S(1)} %get-tuple-element.111), kind=kOutput, calls=%fused_computation.17.clone.1 | convolution fusion | flops 545521664 | bytes 17842176 | tf_op jit(solution)/shard_map/while/body/eval_jaxpr/hqk,khd->qhd/dot_general | solution.py:55
  192.6 4.9 %gather_fusion.1 = bf16[1024,256]{1,0:T(8,128)(2,1)} fusion(bf16[2048,256]{1,0:T(8,128)(2,1)S(1)} %get-tuple-element.133, s32[1024]{0:T(1024)S(1)} %broadcast_clamp_fusion.4), kind=kCustom, calls=%fused_computation.1.clone.1 | custom fusion | bytes 1052672 | tf_op jit(solution)/shard_map/while/body/eval_jaxpr/gather | solution.py:44
  206.7 10.3 %fusion.89 = (f32[4,1024]{1,0:T(4,128)S(1)}, f32[4,1024,1024]{1,2,0:T(8,128)}) fusion(pred[1024]{0:T(1024)(128)(4,1)S(1)} %dynamic-slice_reduce_fusion.2, bf16[1024,4,64]{0,2,1:T(8,128)(2,1)} %bitcast.75, bf16[1024,4,64]{0,2,1:T(8,128)(2,1)} %bitcast.76), kind=kOutput, calls=%fused_computation.105.clone.1 | convolution fusion | flops 553649152 | bytes 17843200 | tf_op jit(solution)/shard_map/while/body/eval_jaxpr/sub | solution.py:53
  217.0 5.9 %gather_fusion = bf16[1024,256]{1,0:T(8,128)(2,1)} fusion(bf16[2048,256]{1,0:T(8,128)(2,1)} %get-tuple-element.131, s32[1024]{0:T(1024)S(1)} %broadcast_clamp_fusion.4), kind=kCustom, calls=%fused_computation.clone.1 | custom fusion | bytes 1052672 | tf_op jit(solution)/shard_map/while/body/eval_jaxpr/gather | solution.py:46
  225.0 8.4 %fusion.90 = bf16[4,64,1024]{2,1,0:T(8,128)(2,1)} fusion(bf16[1024,4,64]{0,2,1:T(8,128)(2,1)} %bitcast.77, f32[4,1024,1024]{1,2,0:T(8,128)} %get-tuple-element.110, f32[4,1024]{1,0:T(4,128)S(1)} %get-tuple-element.111), kind=kOutput, calls=%fused_computation.17.clone.1 | convolution fusion | flops 545521664 | bytes 17842176 | tf_op jit(solution)/shard_map/while/body/eval_jaxpr/hqk,khd->qhd/dot_general | solution.py:55
  237.3 4.9 %gather_fusion.1 = bf16[1024,256]{1,0:T(8,128)(2,1)} fusion(bf16[2048,256]{1,0:T(8,128)(2,1)S(1)} %get-tuple-element.133, s32[1024]{0:T(1024)S(1)} %broadcast_clamp_fusion.4), kind=kCustom, calls=%fused_computation.1.clone.1 | custom fusion | bytes 1052672 | tf_op jit(solution)/shard_map/while/body/eval_jaxpr/gather | solution.py:44
  244.3 4.9 %gather_fusion.2 = bf16[1024,256]{1,0:T(8,128)(2,1)} fusion(bf16[2048,256]{1,0:T(8,128)(2,1)S(1)} %get-tuple-element.134, s32[1024]{0:T(1024)S(1)} %broadcast_clamp_fusion.4), kind=kCustom, calls=%fused_computation.2.clone.1 | custom fusion | bytes 1052672 | tf_op jit(solution)/shard_map/while/body/eval_jaxpr/gather | solution.py:45
  251.4 10.3 %fusion.89 = (f32[4,1024]{1,0:T(4,128)S(1)}, f32[4,1024,1024]{1,2,0:T(8,128)}) fusion(pred[1024]{0:T(1024)(128)(4,1)S(1)} %dynamic-slice_reduce_fusion.2, bf16[1024,4,64]{0,2,1:T(8,128)(2,1)} %bitcast.75, bf16[1024,4,64]{0,2,1:T(8,128)(2,1)} %bitcast.76), kind=kOutput, calls=%fused_computation.105.clone.1 | convolution fusion | flops 553649152 | bytes 17843200 | tf_op jit(solution)/shard_map/while/body/eval_jaxpr/sub | solution.py:53
  261.7 5.9 %gather_fusion = bf16[1024,256]{1,0:T(8,128)(2,1)} fusion(bf16[2048,256]{1,0:T(8,128)(2,1)} %get-tuple-element.131, s32[1024]{0:T(1024)S(1)} %broadcast_clamp_fusion.4), kind=kCustom, calls=%fused_computation.clone.1 | custom fusion | bytes 1052672 | tf_op jit(solution)/shard_map/while/body/eval_jaxpr/gather | solution.py:46
  269.7 8.4 %fusion.90 = bf16[4,64,1024]{2,1,0:T(8,128)(2,1)} fusion(bf16[1024,4,64]{0,2,1:T(8,128)(2,1)} %bitcast.77, f32[4,1024,1024]{1,2,0:T(8,128)} %get-tuple-element.110, f32[4,1024]{1,0:T(4,128)S(1)} %get-tuple-element.111), kind=kOutput, calls=%fused_computation.17.clone.1 | convolution fusion | flops 545521664 | bytes 17842176 | tf_op jit(solution)/shard_map/while/body/eval_jaxpr/hqk,khd->qhd/dot_general | solution.py:55
  282.0 8.5 %gather_fusion.4 = bf16[2048,256]{1,0:T(8,128)(2,1)S(1)} fusion(bf16[4096,256]{1,0:T(8,128)(2,1)} %bitcast.73, s32[2048]{0:T(1024)S(1)} %copy-done.6), kind=kCustom, calls=%fused_computation.4 | custom fusion | bytes 2105344 | tf_op jit(solution)/shard_map/gather | solution.py:60
  293.3 15.8 %reduce-scatter.3.cloned.1.call-done = f32[2048,256]{1,0:T(8,128)} async-done(((f32[2048,512]{1,0:T(8,128)}), f32[2048,256]{1,0:T(8,128)}) %reduce-scatter.3.cloned.1.call-update) | async-done | bytes 2097168 | tf_op jit(solution)/shard_map/reduce_scatter | solution.py:93
  310.8 40.7 %all_to_all.15 = bf16[128,16,256]{2,1,0:T(8,128)(2,1)S(1)} all-to-all(bf16[128,16,256]{2,1,0:T(8,128)(2,1)S(1)} %bitcast.80), channel_id=1, replica_groups=mesh['space'=128,'mp'=2] {'space'}, dimensions={0} | all-to-all | bytes 2097152 | tf_op jit(solution)/shard_map/all_to_all | solution.py:96
  351.5 7.5 %gather_fusion.5 = bf16[2048,256]{1,0:T(8,128)(2,1)S(1)} fusion(bf16[2048,256]{1,0:T(8,128)(2,1)S(1)} %bitcast.72, s32[2048]{0:T(1024)S(1)} %copy-done.5), kind=kCustom, calls=%fused_computation.5 | custom fusion | bytes 2105344 | tf_op jit(solution)/shard_map/gather | solution.py:103
  359.2 8.5 %all_to_all.16 = bf16[2,2048,256]{2,1,0:T(8,128)(2,1)S(1)} all-to-all(bf16[2,2048,256]{2,1,0:T(8,128)(2,1)S(1)} %pad_maximum_fusion), channel_id=1, replica_groups=mesh['space'=128,'mp'=2] {'mp'}, dimensions={0} | all-to-all | bytes 4194304 | tf_op jit(solution)/shard_map/all_to_all | solution.py:105
  371.3 7.3 %fusion.32 = bf16[2048,512]{1,0:T(8,128)(2,1)} fusion(bf16[1024,512]{1,0:T(8,128)(2,1)S(1)} %copy-done, bf16[512,1024]{1,0:T(8,128)(2,1)} %param.18, bf16[2048,512]{1,0:T(8,128)(2,1)S(1)} %get-tuple-element.60, f32[512]{0:T(512)S(1)} %copy-done.11, f32[2048]{0:T(1024)S(1)} %add_rsqrt_fusion, f32[2048]{0:T(1024)S(1)} %broadcast_multiply_fusion), kind=kOutput, calls=%fused_computation.51 | convolution fusion | flops 4320133120 | bytes 6309888 | tf_op jit(solution)/shard_map/dot_general | solution.py:113
  378.6 9.6 %reduce-scatter.5.cloned.1.call-done = bf16[1024,512]{1,0:T(8,128)(2,1)} async-done(((bf16[2048,512]{1,0:T(8,128)(2,1)}), bf16[1024,512]{1,0:T(8,128)(2,1)}) %reduce-scatter.5.cloned.1.call-update) | async-done | bytes 1048592 | tf_op jit(solution)/shard_map/reduce_scatter | solution.py:112
  390.7 17.9 %all-gather.2.cloned.1.call-done = bf16[2048,512]{1,0:T(8,128)(2,1)} async-done(((bf16[1024,512]{1,0:T(8,128)(2,1)}), bf16[2048,512]{1,0:T(8,128)(2,1)}) %all-gather.2.cloned.1.call-update) | async-done | bytes 2097168 | tf_op jit(solution)/shard_map/all_gather | solution.py:120
  (95 shorter events, 74.2 us)
Async XLA Ops:
  6.5 364.7 %copy-start = (bf16[1024,512]{1,0:T(8,128)(2,1)S(1)}, bf16[1024,512]{1,0:T(8,128)(2,1)}, u32[]{:S(2)}) copy-start(bf16[1024,512]{1,0:T(8,128)(2,1)} %param.19) | copy-start | bytes 3145732
  6.5 4.5 %copy-start.7 = (s32[2048]{0:T(1024)S(1)}, s32[2048]{0:T(1024)}, u32[]{:S(2)}) copy-start(s32[2048]{0:T(1024)} %param.12) | copy-start | bytes 24580
  6.5 13.2 %copy-start.8 = (f32[512]{0:T(512)S(1)}, f32[512]{0:T(512)}, u32[]{:S(2)}) copy-start(f32[512]{0:T(512)} %param.14) | copy-start | bytes 6148
  31.1 16.7 %copy-start.9 = (s32[1,4]{1,0:T(1,128)S(1)}, s32[1,4]{1,0:T(1,128)}, u32[]{:S(2)}) copy-start(s32[1,4]{1,0:T(1,128)} %param.13) | copy-start | bytes 52
  31.1 65.8 %all-to-all-start = ((bf16[128,16,512]{2,1,0:T(8,128)(2,1)}), bf16[128,16,512]{2,1,0:T(8,128)(2,1)S(1)}, u32[]{:S(2)}, u32[]{:S(2)}) async-start(bf16[128,16,512]{2,1,0:T(8,128)(2,1)} %bitcast.79), calls=%async_computation | async-start | bytes 4194304 | tf_op jit(solution)/shard_map/all_to_all | solution.py:84
  47.5 261.6 %reduce-scatter.3.cloned.1.call-start = ((), (), s32[]{:S(2)}) async-start(), calls=%async_computation.5 | async-start | bytes 6291456 | tf_op jit(solution)/shard_map/reduce_scatter | solution.py:93
  96.9 1.4 copy-start.2
  98.2 2.5 copy-start.10
  98.2 2.6 copy-start.3
  103.2 178.8 %copy-start.6 = (s32[2048]{0:T(1024)S(1)}, s32[2048]{0:T(1024)}, u32[]{:S(2)}) copy-start(s32[2048]{0:T(1024)} %broadcast_clamp_fusion.1) | copy-start | bytes 24580
  282.0 8.6 %copy-start.4 = (bf16[256,512]{1,0:T(8,128)(2,1)S(1)}, bf16[256,512]{1,0:T(8,128)(2,1)}, u32[]{:S(2)}) copy-start(bf16[256,512]{1,0:T(8,128)(2,1)} %param.16) | copy-start | bytes 786436
  293.2 58.3 %copy-start.5 = (s32[2048]{0:T(1024)S(1)}, s32[2048]{0:T(1024)}, u32[]{:S(2)}) copy-start(s32[2048]{0:T(1024)} %get-tuple-element.61) | copy-start | bytes 24580
  293.2 95.0 %reduce-scatter.5.cloned.1.call-start = ((), (), s32[]{:S(2)}) async-start(), calls=%async_computation.6 | async-start | bytes 3145728 | tf_op jit(solution)/shard_map/reduce_scatter | solution.py:112
  368.0 1.6 copy-start.1
  369.6 1.6 copy-start.11
  378.5 30.1 %all-gather.2.cloned.1.call-start = ((), (), s32[]{:S(2)}) async-start(), calls=%async_computation.7 | async-start | bytes 3145728 | tf_op jit(solution)/shard_map/all_gather | solution.py:120
Sparse Core Ops, SparseCore 0:
  293.4 15.7 reduce-scatter.2
  378.7 9.4 reduce-scatter.4
  390.8 17.7 all-gather.1
